TPU v7x, 32 devices: a whole 2x2x4 slice. The times are simulated.
32 devices in a mesh: batch: 4 (over z), neg: 2 (over y), weight: 4 (over x, core).
Axes of the slice: x: 2, y: 2, z: 4, core: 2. Of those that a mesh axis runs over, the one named last changes fastest.
Arguments:
- images: bfloat16 [1024, 2048], P('batch'), may hold values from -30 to 30
- img_pair: int32 [1024], P('batch'), may hold values from 0 to 1023, each once
- texts: bfloat16 [1024, 2048], P(('batch', 'neg', 'weight')), may hold values from -100 to 100
- txt_pair: int32 [1024], P(('batch', 'neg', 'weight')), may hold values from 0 to 1023, each once
- gain: float32 [2048], replicated, may hold values from 0.1 to 1.9
- perm: int32 [2048], replicated, may hold values from 0 to 2047, each once
- right_blocks: bfloat16 [32, 64, 64], P('weight'), may hold values from -0.75 to 0.75
- left_blocks: bfloat16 [32, 64, 64], P('weight'), may hold values from -0.75 to 0.75
Outputs:
- grad_img: bfloat16 [1024, 2048], P(('batch', 'neg', 'weight'))
- row_loss: float32 [1024], P('batch')
Inputs may be any that keep to these rules, and one draw needn't show every extreme that they name: Every pair id appears once in img_pair and once in txt_pair.
All inputs are finite; a program needn't handle non-finite values.
Results may differ from a plain program's by a relative error of at most 0.0065.
Values may be sent and summed in bfloat16 or wider, within the bound.
A program may use at most 64 MiB of HBM per device.

v0:
```python
import functools
import math

import jax
import jax.numpy as jnp
from jax import lax
from jax.experimental import pallas as pl
from jax.experimental.pallas import tpu as pltpu
from jax.sharding import PartitionSpec as P

LOGIT_GAIN = 2.8
MESH = pl.DeviceIdType.MESH
F32, BF16 = jnp.float32, jnp.bfloat16
PARTS = 1
VMEM_FOR_TEXTS = 16 * 2**20


def plane_orders(count):
    return [sorted(range(count), key=lambda o: (abs(o - own), o)) for own in range(count)]


def block_diagonal(wide):
    size = wide.shape[0]
    lane = lax.broadcasted_iota(jnp.int32, wide.shape, 1)
    values = wide.astype(F32)
    upper = jnp.where(lane < size, values, 0.0)
    lower = jnp.where(lane < size, 0.0, values)
    return jnp.concatenate([upper, lower], axis=0).astype(BF16)


def fused_kernel(
    dims, images_hbm, img_pair_hbm, texts_ref, txt_pair_hbm, gain_hbm, perm_hbm, right_hbm, left_hbm,
    grad_ref, loss_ref, img_pair_ref, txt_pair_ref, gain_ref, perm_ref, right_ref, left_ref,
    rows_ref, wts, buf, pairs, normed_ref, active_ref, permuted_ref, emb_ref, score_ref, losses,
    local_sem, wt_send, wt_recv, send_sem, recv_sem, pair_send, pair_recv, loss_send, loss_recv,
):
    nb, nn, nw = dims
    width = texts_ref.shape[1]
    t_rows = texts_ref.shape[0]
    block_count, size = right_ref.shape[0], right_ref.shape[1]
    pair_count = block_count // 2
    lanes = 2 * size
    r_rows = rows_ref.shape[0]
    group = nn * nw
    b, n, w = lax.axis_index("batch"), lax.axis_index("neg"), lax.axis_index("weight")
    core = lax.rem(w, 2)
    far = 1 - 2 * lax.div(w, 2)
    flip = 1 - 2 * n
    n_a, w_a = n + core * flip, w + (1 - core) * 2 * far
    n_b, w_b = n + (1 - core) * flip, w + core * 2 * far
    n_d, w_d = 1 - n, w + 2 * far
    w_p = w + 1 - 2 * core
    dev_a, dev_b, dev_p = (b, n_a, w_a), (b, n_b, w_b), (b, n, w_p)
    dev_x = (b, n, w_d)
    dev_up, dev_down = (b + 1, n, w), (b - 1, n, w)
    me = n * nw + w

    def slot(o, nn_, ww_):
        return (o * nn + nn_) * nw + ww_

    orders = plane_orders(nb)

    def origin(k):
        value = jnp.int32(orders[0][k])
        for own in range(1, nb):
            value = jnp.where(b == own, orders[own][k], value)
        return value

    planes = [origin(k) for k in range(nb)]

    barrier = pltpu.get_barrier_semaphore()
    near = [dev_a, dev_b, dev_p, (b, n_d, w_d)]
    near += [(b, n_a, w_a + 1 - 2 * core), (b, n_b, w_b + 1 - 2 * core), (b, n_d, w_d + 1 - 2 * core)]
    for dev in near:
        pl.semaphore_signal(barrier, inc=1, device_id=dev, device_id_type=MESH)

    @pl.when(b < nb - 1)
    def _():
        pl.semaphore_signal(barrier, inc=1, device_id=dev_up, device_id_type=MESH)

    @pl.when(b > 0)
    def _():
        pl.semaphore_signal(barrier, inc=1, device_id=dev_down, device_id_type=MESH)

    own_slot = slot(b, n, w)
    staged = [
        pltpu.make_async_copy(source, target, local_sem.at[2 + i])
        for i, (source, target) in enumerate([
            (right_hbm, right_ref), (left_hbm, left_ref), (txt_pair_hbm, txt_pair_ref),
            (gain_hbm, gain_ref), (perm_hbm, perm_ref), (img_pair_hbm, img_pair_ref),
        ])
    ]
    for copy in staged:
        copy.start()
    copy_rows = pltpu.make_async_copy(images_hbm.at[pl.ds(pl.multiple_of(me * r_rows, r_rows), r_rows)], rows_ref, local_sem.at[0])
    copy_text = pltpu.make_async_copy(texts_ref, buf.at[own_slot], local_sem.at[1])
    copy_rows.start()
    copy_text.start()
    expected = len(near) + jnp.where(b < nb - 1, 1, 0) + jnp.where(b > 0, 1, 0)
    pl.semaphore_wait(barrier, expected)

    def weight_copy(index, kind, dev):
        return pltpu.make_async_remote_copy(
            src_ref=wts.at[index], dst_ref=wts.at[index], send_sem=wt_send.at[kind], recv_sem=wt_recv.at[index],
            device_id=dev, device_id_type=MESH,
        )

    half = t_rows // PARTS

    def text_copy(index, kind, part, dev, source):
        rows = pl.ds(part * half, half)
        return pltpu.make_async_remote_copy(
            src_ref=source.at[rows], dst_ref=buf.at[index, rows], send_sem=send_sem.at[index, kind, part],
            recv_sem=recv_sem.at[index, part], device_id=dev, device_id_type=MESH,
        )

    def pair_copy(index, kind, dev):
        return pltpu.make_async_remote_copy(
            src_ref=pairs.at[index], dst_ref=pairs.at[index], send_sem=pair_send.at[index, kind],
            recv_sem=pair_recv.at[index], device_id=dev, device_id_type=MESH,
        )

    sent = []

    def launch(copy, when):
        if when is None:
            copy.start()
            sent.append(copy.wait_send)
        else:
            pl.when(when)(copy.start)
            sent.append(lambda: pl.when(when)(copy.wait_send))

    def send_text(index, kind, part, dev, source, when):
        launch(text_copy(index, kind, part, dev, source), when)

    def send_pair(index, kind, dev, when):
        launch(pair_copy(index, kind, dev), when)

    def send(index, kind, part, dev, when=None):
        send_text(index, kind, part, dev, buf.at[index], when)
        if part == PARTS - 1:
            send_pair(index, kind, dev, when)

    def arrive(index, part):
        text_copy(index, 0, part, dev_a, buf.at[index]).wait_recv()
        if part == PARTS - 1:
            pair_copy(index, 0, dev_a).wait_recv()

    def along_chain(o, receiver):
        distance = jnp.abs(o - receiver)
        return distance < 0

    def column(k):
        o = planes[k]
        index = slot(o, n, w)
        for part in range(PARTS):
            arrive(index, part)
            send(index, 3, part, dev_up, (o <= b) & (b < nb - 1))
            send(index, 4, part, dev_down, (o >= b) & (b > 0))
            send(index, 0, part, dev_a)
            send(index, 1, part, dev_b)
            send(index, 2, part, dev_p)

    def from_a(k):
        index = slot(planes[k], n_a, w_a)
        for part in range(PARTS):
            arrive(index, part)
            send(index, 1, part, dev_b, jnp.logical_not(along_chain(planes[k], b)) if k else None)
            send(index, 2, part, dev_p)

    def from_b(k):
        index = slot(planes[k], n_b, w_b)
        for part in range(PARTS):
            arrive(index, part)
            send(index, 2, part, dev_p)

    def diagonal(k):
        o = planes[k]
        index = slot(o, n_d, w_d)
        for part in range(PARTS):
            arrive(index, part)
            send(index, 3, part, dev_up, (o <= b) & (b < nb - 1) & along_chain(o, b + 1))
            send(index, 4, part, dev_down, (o >= b) & (b > 0) & along_chain(o, b - 1))
            send(index, 2, part, dev_p)

    def from_partner(k):
        for nn_ in range(nn):
            for ww_ in range(nw // 2):
                for part in range(PARTS):
                    arrive(slot(planes[k], nn_, 2 * ww_ + 1 - core), part)

    own_targets = [
        (3, dev_up, b < nb - 1), (4, dev_down, b > 0), (0, dev_a, None), (1, dev_b, None), (2, dev_p, None),
    ]

    def own_sends(part):
        for kind, dev, when in own_targets:
            send_text(own_slot, kind, part, dev, texts_ref, when)

    def layer_norm():
        copy_rows.wait()
        for copy in staged[3:]:
            copy.wait()
        values = rows_ref[...].astype(F32)
        mean = jnp.sum(values, axis=1, keepdims=True) / width
        centered = values - mean
        var = jnp.sum(centered * centered, axis=1, keepdims=True) / width
        normed_ref[...] = (centered * lax.rsqrt(var + 1e-05) * gain_ref[...]).astype(BF16)

    for part in range(PARTS):
        own_sends(part)

    for copy in staged[:3]:
        copy.wait()
    ids = txt_pair_ref[...]
    pairs[own_slot] = jnp.concatenate([ids] * nw, axis=1)
    for k in range(pair_count):
        wts[w, k] = jnp.concatenate([right_ref[2 * k], right_ref[2 * k + 1]], axis=1)
        wts[w, pair_count + k] = jnp.concatenate([left_ref[2 * k], left_ref[2 * k + 1]], axis=1)
    layer_norm()
    for kind, dev, when in own_targets:
        send_pair(own_slot, kind, dev, when)
    weight_copy(w, 0, dev_x).start()
    weight_copy(w, 1, dev_p).start()

    column(1)
    from_a(0)
    from_b(0)
    column(2)
    from_a(1)
    weight_copy(w_d, 0, dev_x).wait_recv()
    weight_copy(w_d, 2, dev_p).start()
    for k in range(3, nb):
        column(k)
    diagonal(0)
    from_b(1)
    from_a(2)
    weight_copy(w_p, 0, dev_x).wait_recv()
    weight_copy(w_d + 1 - 2 * core, 0, dev_x).wait_recv()
    diagonal(1)
    from_b(2)

    for s in range(nw):
        for k in range(pair_count):
            at = (s * pair_count + k) * lanes
            inner = jnp.dot(
                normed_ref[:, at : at + lanes], block_diagonal(wts[s, k]), preferred_element_type=F32
            )
            active_ref[:, at : at + lanes] = jax.nn.gelu(inner, approximate=True).astype(BF16)

    step = 2 * lanes
    row_id = lax.broadcasted_iota(jnp.int32, (width, step), 0)

    def permute(lo, hi):
        @pl.loop(lo, hi)
        def _(c):
            at = pl.ds(pl.multiple_of(c * step, step), step)
            chosen = jnp.where(row_id == perm_ref[:, at], 1.0, 0.0).astype(BF16)
            permuted_ref[:, at] = jnp.dot(active_ref[...], chosen, preferred_element_type=F32).astype(BF16)

    chunks = width // step
    for k in range(3, nb):
        from_a(k)
    permute(0, chunks // 2)
    for k in range(3, nb):
        from_b(k)
    permute(chunks // 2, chunks)

    for s in range(nw):
        for k in range(pair_count):
            at = (s * pair_count + k) * lanes
            outer = jnp.dot(
                permuted_ref[:, at : at + lanes], block_diagonal(wts[s, pair_count + k]), preferred_element_type=F32
            )
            emb_ref[:, at : at + lanes] = (rows_ref[:, at : at + lanes].astype(F32) + outer).astype(BF16)

    logit_scale = LOGIT_GAIN / math.sqrt(width)
    copy_text.wait()

    def scores(k):
        from_partner(k)
        block = buf[pl.ds(planes[k] * group, group)].reshape(group * t_rows, width)
        product = lax.dot_general(emb_ref[...], block, (((1,), (1,)), ((), ())), preferred_element_type=F32)
        score_ref[planes[k]] = product * logit_scale

    scores(0)
    diagonal(2)
    scores(1)
    for k in range(3, nb):
        diagonal(k)
    for k in range(2, nb):
        scores(k)

    columns = group * t_rows
    total_rows = img_pair_ref.shape[1]
    place = lax.broadcasted_iota(jnp.int32, (r_rows, total_rows), 1) == (
        lax.broadcasted_iota(jnp.int32, (r_rows, total_rows), 0) + me * r_rows
    )
    own_ids = jnp.sum(jnp.where(place, img_pair_ref[...], 0), axis=1, keepdims=True)
    quarter = lax.broadcasted_iota(jnp.int32, (1, nw * t_rows), 1) // t_rows

    def pair_row(first):
        row = pairs[first]
        for ww_ in range(1, nw):
            row = jnp.where(quarter == ww_, pairs[first + ww_], row)
        return row

    found = [
        own_ids == jnp.concatenate([pair_row(slot(o, nn_, 0)) for nn_ in range(nn)], axis=1) for o in range(nb)
    ]
    parts = [score_ref[o] for o in range(nb)]
    row_max = functools.reduce(jnp.maximum, [jnp.max(part, axis=1, keepdims=True) for part in parts])
    shifted = [jnp.exp(part - row_max) for part in parts]
    totals = functools.reduce(jnp.add, [jnp.sum(part, axis=1, keepdims=True) for part in shifted])
    positive = functools.reduce(
        jnp.add, [jnp.sum(jnp.where(hit, part, 0.0), axis=1, keepdims=True) for hit, part in zip(found, parts)]
    )
    row_loss = row_max + jnp.log(totals) - positive
    losses[me] = jnp.sum(jnp.where(place, row_loss, 0.0), axis=0, keepdims=True)
    dscore = [
        (part / totals - jnp.where(hit, 1.0, 0.0)).astype(BF16) for hit, part in zip(found, shifted)
    ]

    tile = width // 8

    def gradient(c):
        at = slice(c * tile, (c + 1) * tile)
        total = jnp.zeros((r_rows, tile), F32)
        for o in range(nb):
            block = buf[o * group : (o + 1) * group, :, at].reshape(columns, tile)
            total = total + jnp.dot(dscore[o], block, preferred_element_type=F32)
        grad_ref[:, at] = total.astype(BF16)

    gradient(0)
    loss_copies = []
    for position, dev in enumerate(near):
        loss_copies.append(
            pltpu.make_async_remote_copy(
                src_ref=losses.at[me], dst_ref=losses.at[me], send_sem=loss_send.at[position],
                recv_sem=loss_recv.at[me], device_id=dev, device_id_type=MESH,
            )
        )
        loss_copies[-1].start()
    for c in range(1, 8):
        gradient(c)
    for _, n_o, w_o in near:
        other = n_o * nw + w_o
        pltpu.make_async_remote_copy(
            src_ref=losses.at[other], dst_ref=losses.at[other], send_sem=loss_send.at[0],
            recv_sem=loss_recv.at[other], device_id=dev_p, device_id_type=MESH,
        ).wait_recv()
    loss_ref[...] = functools.reduce(jnp.add, [losses[i] for i in range(group)])

    for finish in sent:
        finish()
    weight_copy(w, 0, dev_x).wait_send()
    weight_copy(w, 1, dev_p).wait_send()
    weight_copy(w_d, 2, dev_p).wait_send()
    for copy in loss_copies:
        copy.wait_send()


def fused(dims, images, img_pair, texts, txt_pair, gain, perm, right_blocks, left_blocks):
    nb, nn, nw = dims
    group = nn * nw
    devices = nb * group
    t_rows, width = texts.shape
    r_rows = images.shape[0] // group
    block_count, size = right_blocks.shape[:2]
    vmem = pl.BlockSpec(memory_space=pltpu.VMEM)
    hbm = pl.BlockSpec(memory_space=pltpu.HBM)
    dma = pltpu.SemaphoreType.DMA
    grad, loss = pl.pallas_call(
        functools.partial(fused_kernel, dims),
        out_shape=(
            jax.ShapeDtypeStruct((r_rows, width), BF16),
            jax.ShapeDtypeStruct((1, images.shape[0]), F32),
        ),
        in_specs=[hbm] * 8,
        out_specs=(vmem, vmem),
        scratch_shapes=[
            pltpu.VMEM((1, images.shape[0]), jnp.int32),
            pltpu.VMEM((1, t_rows), jnp.int32),
            pltpu.VMEM((1, width), F32),
            pltpu.VMEM((1, width), jnp.int32),
            pltpu.VMEM(right_blocks.shape, BF16),
            pltpu.VMEM(left_blocks.shape, BF16),
            pltpu.VMEM((r_rows, width), BF16),
            pltpu.VMEM((nw, block_count, size, 2 * size), BF16),
            pltpu.VMEM((devices, t_rows, width), BF16),
            pltpu.VMEM((devices, 1, nw * t_rows), jnp.int32),
            pltpu.VMEM((r_rows, width), BF16),
            pltpu.VMEM((r_rows, width), BF16),
            pltpu.VMEM((r_rows, width), BF16),
            pltpu.VMEM((r_rows, width), BF16),
            pltpu.VMEM((nb, r_rows, group * t_rows), F32),
            pltpu.VMEM((group, 1, images.shape[0]), F32),
            dma((8,)),
            dma((3,)),
            dma((nw,)),
            dma((devices, 5, PARTS)),
            dma((devices, PARTS)),
            dma((devices, 5)),
            dma((devices,)),
            dma((group - 1,)),
            dma((group,)),
        ],
        compiler_params=pltpu.CompilerParams(
            collective_id=0, has_side_effects=True, vmem_limit_bytes=67_043_328
        ),
    )(
        images, img_pair[None], texts, txt_pair[None], gain[None], perm[None], right_blocks, left_blocks
    )
    return grad, loss[0]


def monarch(images, gain, perm, right_full, left_full):
    row_count, width = images.shape
    block_count, block_size = (right_full.shape[0], right_full.shape[1])
    values = images.astype(jnp.float32)
    row_mean = jnp.mean(values, axis=1, keepdims=True)
    centered = values - row_mean
    row_var = jnp.mean(centered * centered, axis=1, keepdims=True)
    normed = (centered * lax.rsqrt(row_var + 1e-05) * gain).astype(jnp.bfloat16)
    inner_mixed = jnp.einsum(
        "rke,kec->rkc",
        normed.reshape(row_count, block_count, block_size),
        right_full,
        preferred_element_type=jnp.float32,
    )
    active = (
        jax.nn.gelu(inner_mixed, approximate=True).astype(jnp.bfloat16).reshape(row_count, width)
    )
    permuted = jnp.take(active, perm, axis=1)
    outer_mixed = jnp.einsum(
        "rke,kec->rkc",
        permuted.reshape(row_count, block_count, block_size),
        left_full,
        preferred_element_type=jnp.float32,
    )
    return (values + outer_mixed.reshape(row_count, width)).astype(jnp.bfloat16)


def per_device(images, img_pair, texts, txt_pair, gain, perm, right_blocks, left_blocks):
    right_full, left_full = (
        lax.all_gather(right_blocks, "weight", axis=0, tiled=True),
        lax.all_gather(left_blocks, "weight", axis=0, tiled=True),
    )
    embedded = monarch(images, gain, perm, right_full, left_full)
    gathered, gathered_pair = (
        lax.all_gather(texts, "batch", axis=0, tiled=True),
        lax.all_gather(txt_pair, "batch", axis=0, tiled=True),
    )
    logit_scale = LOGIT_GAIN / math.sqrt(images.shape[1])
    scores = (
        jnp.einsum("rd,cd->rc", embedded, gathered, preferred_element_type=jnp.float32)
        * logit_scale
    )
    matches = (img_pair[:, None] == gathered_pair[None, :]).astype(jnp.float32)
    local_max = jnp.max(scores, axis=1)
    local_pos = jnp.sum(matches * scores, axis=1)
    row_max = lax.pmax(local_max, ("neg", "weight"))
    shifted = jnp.exp(scores - row_max[:, None])
    totals, positive = lax.psum((jnp.sum(shifted, axis=1), local_pos), ("neg", "weight"))
    row_loss = row_max + jnp.log(totals) - positive
    dscore = (shifted / totals[:, None] - matches).astype(jnp.bfloat16)
    grad_sum = lax.psum_scatter(
        jnp.dot(dscore, gathered, preferred_element_type=jnp.float32),
        ("neg", "weight"),
        scatter_dimension=0,
        tiled=True,
    )
    grad_img = grad_sum.astype(jnp.bfloat16)
    return (grad_img, row_loss)


def solution(mesh):
    dims = tuple(mesh.shape[axis] for axis in ("batch", "neg", "weight"))

    def body(images, img_pair, texts, txt_pair, gain, perm, right_blocks, left_blocks):
        args = (images, img_pair, texts, txt_pair, gain, perm, right_blocks, left_blocks)
        text_bytes = math.prod(dims) * texts.size * texts.dtype.itemsize
        if dims[1:] == (2, 4) and dims[0] >= 3 and texts.shape[0] % (16 * PARTS) == 0 and text_bytes <= VMEM_FOR_TEXTS:
            return fused(dims, *args)
        return per_device(*args)

    return jax.shard_map(
        body,
        mesh=mesh,
        in_specs=(
            P("batch", None),
            P("batch"),
            P(("batch", "neg", "weight"), None),
            P(("batch", "neg", "weight")),
            P(),
            P(),
            P("weight", None, None),
            P("weight", None, None),
        ),
        out_specs=(P(("batch", "neg", "weight"), None), P("batch")),
        check_vma=False,
    )
```

profile of v0, /device:TPU:0, one launch (start us, length us, event | category | flops | bytes accessed | tf_op | source)
XLA Modules:
  0.0 41.3 jit_solution(1933072449511344607)
XLA Ops:
  0.6 38.5 %shard_map.95 = (bf16[32,2048]{1,0:T(8,128)(2,1)}, f32[1,256]{1,0:T(1,128)}) custom-call(bf16[256,2048]{1,0:T(8,128)(2,1)} %images_hbm.1, s32[1,256]{1,0:T(1,128)} %bitcast.7, bf16[32,2048]{1,0:T(8,128)(2,1)} %texts_ref.1, s32[1,32]{1,0:T(1,128)} %bitcast.9, f32[1,2048]{1,0:T(1,128)} %bitcast.5, s32[1,2048]{1,0:T(1,128)} %bitcast.6, ...), custom_call_target="tpu_custom_call" | custom-call | tf_op jit(solution)/shard_map/pallas_call | solution.py:373
  39.2 0.0 copy-start
  39.2 1.6 %copy.12 = bf16[32,2048]{1,0:T(8,128)(2,1)} copy(bf16[32,2048]{1,0:T(8,128)(2,1)} %get-tuple-element.8) | data formatting | bytes 262144
  40.8 0.0 copy-done
  40.8 0.6 %copy.13 = f32[256]{0:T(256)} copy(f32[256]{0:T(256)S(1)} %bitcast.8) | data formatting | bytes 2048
Async XLA Ops:
  39.2 1.6 %copy-start = (f32[1,256]{1,0:T(1,128)S(1)}, f32[1,256]{1,0:T(1,128)}, u32[]{:S(2)}) copy-start(f32[1,256]{1,0:T(1,128)} %get-tuple-element.5) | copy-start | bytes 3076
where the time goes:
time: 41.5 us; the launch traced here: 41.3 us
  Pallas kernels  38.5 us (93%)
  local copies, waits for them, and re-layouts  2.14 us (5%)
  between operations  0.65 us (2%)
    pallas_call x1, Pallas kernels, fused(): pl.pallas_call(functools.partial(fused_kernel, dims), out_shape=(jax.Shap...  38.5 us
    unnamed x4, local copies, waits for them, and re-layouts  2.14 us

commit v1 on v0

v1 whole, which is shorter than its diff:
```python
import functools
import math

import jax
import jax.numpy as jnp
from jax import lax
from jax.experimental import pallas as pl
from jax.experimental.pallas import tpu as pltpu
from jax.sharding import PartitionSpec as P

LOGIT_GAIN = 2.8
MESH = pl.DeviceIdType.MESH
F32, BF16 = jnp.float32, jnp.bfloat16
PARTS = 2
VMEM_LIMIT = 67_043_328


def plane_orders(count):
    return [sorted(range(count), key=lambda o: (abs(o - own), o)) for own in range(count)]


def block_diagonal(wide):
    size = wide.shape[0]
    lane = lax.broadcasted_iota(jnp.int32, wide.shape, 1)
    values = wide.astype(F32)
    upper = jnp.where(lane < size, values, 0.0)
    lower = jnp.where(lane < size, 0.0, values)
    return jnp.concatenate([upper, lower], axis=0).astype(BF16)


def fused_kernel(
    dims, images_hbm, img_pair_hbm, texts_ref, txt_pair_hbm, gain_hbm, perm_hbm, right_hbm, left_hbm,
    grad_ref, loss_ref, img_pair_ref, txt_pair_ref, gain_ref, perm_ref, right_ref, left_ref,
    rows_ref, wts, buf, pairs, normed_ref, active_ref, permuted_ref, emb_ref, score_ref, dscore_ref, stats,
    partial_ref, peer_ref, own_ref,
    local_sem, wt_send, wt_recv, send_sem, recv_sem, pair_send, pair_recv, stat_send, stat_recv, part_send, part_recv,
):
    nb, nn, nw = dims
    width = texts_ref.shape[1]
    t_rows = texts_ref.shape[0]
    block_count, size = right_ref.shape[0], right_ref.shape[1]
    pair_count = block_count // 2
    lanes = 2 * size
    two = rows_ref.shape[0]
    r_rows = two // 2
    b, n, w = lax.axis_index("batch"), lax.axis_index("neg"), lax.axis_index("weight")
    core = lax.rem(w, 2)
    across = lax.div(w, 2)
    far = 1 - 2 * across
    flip = 1 - 2 * n
    n_a, w_a = n + core * flip, w + (1 - core) * 2 * far
    n_b, w_b = n + (1 - core) * flip, w + core * 2 * far
    n_d, w_d = 1 - n, w + 2 * far
    other = 1 - 2 * core
    w_p = w + other
    dev_a, dev_b, dev_p = (b, n_a, w_a), (b, n_b, w_b), (b, n, w_p)
    dev_ap = (b, n_a, w_a + other)
    dev_x = (b, n, w_d)
    dev_up, dev_down = (b + 1, n, w), (b - 1, n, w)
    me = n * nw + w
    side = core * n + (1 - core) * across
    spread = core * nw + (1 - core) * 2
    low = me - side * spread
    high = low + spread

    orders = plane_orders(nb)

    def by_plane(values):
        value = jnp.int32(values[0])
        for own in range(1, nb):
            value = jnp.where(b == own, values[own], value)
        return value

    planes = [by_plane([orders[own][k] for own in range(nb)]) for k in range(nb)]

    barrier = pltpu.get_barrier_semaphore()
    near = [dev_a, dev_b, dev_p, (b, n_d, w_d)]
    near += [dev_ap, (b, n_b, w_b + other), (b, n_d, w_d + other)]
    for dev in near:
        pl.semaphore_signal(barrier, inc=1, device_id=dev, device_id_type=MESH)

    @pl.when(b < nb - 1)
    def _():
        pl.semaphore_signal(barrier, inc=1, device_id=dev_up, device_id_type=MESH)

    @pl.when(b > 0)
    def _():
        pl.semaphore_signal(barrier, inc=1, device_id=dev_down, device_id_type=MESH)

    staged = [
        pltpu.make_async_copy(source, target, local_sem.at[3 + i])
        for i, (source, target) in enumerate([
            (right_hbm, right_ref), (left_hbm, left_ref), (txt_pair_hbm, txt_pair_ref),
            (gain_hbm, gain_ref), (perm_hbm, perm_ref), (img_pair_hbm, img_pair_ref),
        ])
    ]
    for copy in staged:
        copy.start()
    copy_rows = [
        pltpu.make_async_copy(
            images_hbm.at[pl.ds(pl.multiple_of(block * r_rows, r_rows), r_rows)],
            rows_ref.at[pl.ds(i * r_rows, r_rows)], local_sem.at[i],
        )
        for i, block in enumerate([low, high])
    ]
    copy_text = pltpu.make_async_copy(texts_ref, buf.at[b, 0], local_sem.at[2])
    for copy in copy_rows:
        copy.start()
    copy_text.start()
    expected = len(near) + jnp.where(b < nb - 1, 1, 0) + jnp.where(b > 0, 1, 0)
    pl.semaphore_wait(barrier, expected)

    def weight_copy(index, kind, dev):
        return pltpu.make_async_remote_copy(
            src_ref=wts.at[index], dst_ref=wts.at[index], send_sem=wt_send.at[kind], recv_sem=wt_recv.at[index],
            device_id=dev, device_id_type=MESH,
        )

    half = t_rows // PARTS

    targets = [(0, 3, dev_up), (0, 4, dev_down), (2, 0, dev_b), (3, 1, dev_ap), (1, 2, dev_p)]

    def text_copy(o, role, kind, part, dev, source):
        rows = pl.ds(pl.multiple_of(part * half, half), half)
        return pltpu.make_async_remote_copy(
            src_ref=source.at[rows], dst_ref=buf.at[o, role, rows], send_sem=send_sem.at[o, kind, part],
            recv_sem=recv_sem.at[o, role, part], device_id=dev, device_id_type=MESH,
        )

    def pair_copy(o, role, kind, dev):
        return pltpu.make_async_remote_copy(
            src_ref=pairs.at[o, 0], dst_ref=pairs.at[o, role], send_sem=pair_send.at[o, kind],
            recv_sem=pair_recv.at[o, role], device_id=dev, device_id_type=MESH,
        )

    sent = []

    def launch(copy, when):
        if when is None:
            copy.start()
            sent.append(copy.wait_send)
        else:
            pl.when(when)(copy.start)
            sent.append(lambda: pl.when(when)(copy.wait_send))

    def onward(kind, o):
        if kind == 3:
            return (o <= b) & (b < nb - 1)
        if kind == 4:
            return (o >= b) & (b > 0)
        return None

    def spread_text(o, part, source):
        for role, kind, dev in targets:
            launch(text_copy(o, role, kind, part, dev, source), onward(kind, o))

    def spread_pair(o):
        for role, kind, dev in targets:
            launch(pair_copy(o, role, kind, dev), onward(kind, o))

    def column(k, part):
        o = planes[k] if isinstance(k, int) else k
        text_copy(o, 0, 0, part, dev_b, buf.at[o, 0]).wait_recv()
        spread_text(o, part, buf.at[o, 0])

    def column_pair(k):
        o = planes[k]
        pair_copy(o, 0, 0, dev_b).wait_recv()
        spread_pair(o)

    def arrive(k):
        o = planes[k]
        for role in (1, 2, 3):
            for part in range(PARTS):
                text_copy(o, role, 0, part, dev_b, buf.at[o, 0]).wait_recv()
            pair_copy(o, role, 0, dev_b).wait_recv()

    for part in range(PARTS):
        spread_text(b, part, texts_ref)

    for copy in staged[:3]:
        copy.wait()
    pairs[b, 0] = jnp.concatenate([txt_pair_ref[...]] * 4, axis=1)
    for k in range(pair_count):
        wts[w, k] = jnp.concatenate([right_ref[2 * k], right_ref[2 * k + 1]], axis=1)
        wts[w, pair_count + k] = jnp.concatenate([left_ref[2 * k], left_ref[2 * k + 1]], axis=1)
    for copy in copy_rows:
        copy.wait()
    for copy in staged[3:]:
        copy.wait()
    weight_copy(w, 0, dev_x).start()
    weight_copy(w, 1, dev_p).start()
    spread_pair(b)

    values = rows_ref[...].astype(F32)
    mean = jnp.sum(values, axis=1, keepdims=True) / width
    centered = values - mean
    var = jnp.sum(centered * centered, axis=1, keepdims=True) / width
    normed_ref[...] = (centered * lax.rsqrt(var + 1e-05) * gain_ref[...]).astype(BF16)

    lane = lax.broadcasted_iota(jnp.int32, (two, img_pair_ref.shape[1]), 1)
    row = lax.broadcasted_iota(jnp.int32, (two, img_pair_ref.shape[1]), 0)
    place = lane == jnp.where(row < r_rows, low * r_rows + row, high * r_rows + row - r_rows)
    own_ids = jnp.sum(jnp.where(place, img_pair_ref[...], 0), axis=1, keepdims=True)

    def first_stage(s):
        for k in range(pair_count):
            at = pl.ds(pl.multiple_of((s * pair_count + k) * lanes, lanes), lanes)
            inner = jnp.dot(normed_ref[:, at], block_diagonal(wts[s, k]), preferred_element_type=F32)
            active_ref[:, at] = jax.nn.gelu(inner, approximate=True).astype(BF16)

    def second_stage(s):
        for k in range(pair_count):
            at = slice((s * pair_count + k) * lanes, (s * pair_count + k + 1) * lanes)
            outer = jnp.dot(
                permuted_ref[:, at], block_diagonal(wts[s, pair_count + k]), preferred_element_type=F32
            )
            emb_ref[:, at] = (rows_ref[:, at].astype(F32) + outer).astype(BF16)

    step = 2 * lanes
    row_id = lax.broadcasted_iota(jnp.int32, (width, step), 0)

    def permute(lo, hi):
        @pl.loop(lo, hi)
        def _(c):
            at = pl.ds(pl.multiple_of(c * step, step), step)
            chosen = jnp.where(row_id == perm_ref[:, at], 1.0, 0.0).astype(BF16)
            permuted_ref[:, at] = jnp.dot(active_ref[...], chosen, preferred_element_type=F32).astype(BF16)

    chunks = width // step
    middle = (b > 0) & (b < nb - 1)
    relays = [(k, part) for k in range(1, nb) for part in range(PARTS)]
    swapped = list(relays)
    if nb > 2 and PARTS == 2:
        swapped[1], swapped[2] = relays[2], relays[1]

    def relay(i):
        if i >= len(relays):
            return
        k, part = relays[i]
        if relays[i] == swapped[i]:
            column(k, part)
        else:
            k2, part2 = swapped[i]
            column(jnp.where(middle, planes[k2], planes[k]), jnp.where(middle, part2, part))

    first_stage(w)
    relay(0)
    weight_copy(w_p, 0, dev_x).wait_recv()
    first_stage(w_p)
    relay(1)
    relay(2)
    weight_copy(w_d, 0, dev_x).wait_recv()
    weight_copy(w_d, 2, dev_p).start()
    first_stage(w_d)
    relay(3)
    column_pair(1)
    w_dp = w_d + other
    weight_copy(w_dp, 0, dev_x).wait_recv()
    first_stage(w_dp)
    permute(0, chunks // 4)
    relay(4)
    permute(chunks // 4, chunks // 2)
    column_pair(2)
    relay(5)
    permute(chunks // 2, 3 * chunks // 4)
    for i in range(6, len(relays)):
        relay(i)
    for k in range(3, nb):
        column_pair(k)
    permute(3 * chunks // 4, chunks)
    for s in range(nw):
        second_stage(s)

    logit_scale = LOGIT_GAIN / math.sqrt(width)
    copy_text.wait()
    columns = 4 * t_rows

    def scores(k):
        if k:
            arrive(k)
        else:
            o = planes[0]
            for role in (1, 2, 3):
                for part in range(PARTS):
                    text_copy(o, role, 0, part, dev_b, buf.at[o, 0]).wait_recv()
                pair_copy(o, role, 0, dev_b).wait_recv()
        block = buf[planes[k]].reshape(columns, width)
        product = lax.dot_general(emb_ref[...], block, (((1,), (1,)), ((), ())), preferred_element_type=F32)
        score_ref[planes[k]] = product * logit_scale

    for k in range(nb):
        scores(k)

    quarter = lax.broadcasted_iota(jnp.int32, (1, columns), 1) // t_rows

    def pair_row(o):
        ids = pairs[o, 0]
        for role in range(1, 4):
            ids = jnp.where(quarter == role, pairs[o, role], ids)
        return ids

    found = [own_ids == pair_row(o) for o in range(nb)]
    parts = [score_ref[o] for o in range(nb)]
    row_max = jnp.max(functools.reduce(jnp.maximum, parts), axis=1, keepdims=True)
    totals = jnp.sum(
        functools.reduce(jnp.add, [jnp.exp(part - row_max) for part in parts]), axis=1, keepdims=True
    )
    positive = jnp.sum(
        functools.reduce(jnp.add, [jnp.where(hit, part, 0.0) for hit, part in zip(found, parts)]),
        axis=1, keepdims=True,
    )
    seat = lax.broadcasted_iota(jnp.int32, (two, stats.shape[2]), 0) == lax.broadcasted_iota(
        jnp.int32, (two, stats.shape[2]), 1
    )

    def to_row(value):
        return jnp.sum(jnp.where(seat, value, 0.0), axis=0, keepdims=True)

    def to_column(value):
        return jnp.sum(jnp.where(seat, value, 0.0), axis=1, keepdims=True)

    stats[me] = jnp.concatenate(
        [to_row(row_max), to_row(totals), to_row(positive), jnp.zeros((5, stats.shape[2]), F32)], axis=0
    )

    def stat_copy(index, position, dev):
        return pltpu.make_async_remote_copy(
            src_ref=stats.at[index], dst_ref=stats.at[index], send_sem=stat_send.at[position],
            recv_sem=stat_recv.at[index], device_id=dev, device_id_type=MESH,
        )

    for position, dev in enumerate(near):
        stat_copy(me, position, dev).start()
    peer = n_a * nw + w_a
    stat_copy(peer, 0, dev_a).wait_recv()
    theirs = stats[peer]
    peer_max = to_column(theirs[0:1])
    peer_totals = to_column(theirs[1:2])
    full_max = jnp.maximum(row_max, peer_max)
    full_totals = totals * jnp.exp(row_max - full_max) + peer_totals * jnp.exp(peer_max - full_max)
    for o in range(nb):
        dscore_ref[:, o * columns : (o + 1) * columns] = (
            jnp.exp(parts[o] - full_max) / full_totals - jnp.where(found[o], 1.0, 0.0)
        ).astype(BF16)

    tiles = partial_ref.shape[0]
    tile = width // tiles

    def gradient(first, c):
        block = buf[:, :, :, c * tile : (c + 1) * tile].reshape(nb * columns, tile)
        return jnp.dot(
            dscore_ref[pl.ds(pl.multiple_of(first, r_rows), r_rows)], block, preferred_element_type=F32
        )

    def part_copy(c):
        return pltpu.make_async_remote_copy(
            src_ref=partial_ref.at[c], dst_ref=peer_ref.at[c], send_sem=part_send.at[c],
            recv_sem=part_recv.at[c], device_id=dev_a, device_id_type=MESH,
        )

    for c in range(tiles):
        partial_ref[c] = gradient((1 - side) * r_rows, c).astype(BF16)
        part_copy(c).start()
    for c in range(tiles):
        own_ref[c] = gradient(side * r_rows, c)

    for _, n_o, w_o in near[1:]:
        stat_copy(n_o * nw + w_o, 0, dev_a).wait_recv()

    def pair_loss(one, two_):
        first, second = stats[one], stats[two_]
        top = jnp.maximum(first[0:1], second[0:1])
        total = first[1:2] * jnp.exp(first[0:1] - top) + second[1:2] * jnp.exp(second[0:1] - top)
        return top + jnp.log(total) - (first[2:3] + second[2:3])

    losses = {}
    for n_o in range(nn):
        both = pair_loss(n_o * nw, n_o * nw + 2)
        losses[n_o * nw], losses[n_o * nw + 2] = both[:, :r_rows], both[:, r_rows:two]
    for x_o in range(2):
        both = pair_loss(2 * x_o + 1, nw + 2 * x_o + 1)
        losses[2 * x_o + 1], losses[nw + 2 * x_o + 1] = both[:, :r_rows], both[:, r_rows:two]
    loss_ref[...] = jnp.concatenate([losses[i] for i in range(nn * nw)], axis=1)

    for c in range(tiles):
        part_copy(c).wait_recv()
        grad_ref[:, c * tile : (c + 1) * tile] = (own_ref[c] + peer_ref[c].astype(F32)).astype(BF16)

    for finish in sent:
        finish()
    weight_copy(w, 0, dev_x).wait_send()
    weight_copy(w, 1, dev_p).wait_send()
    weight_copy(w_d, 2, dev_p).wait_send()
    for position, dev in enumerate(near):
        stat_copy(me, position, dev).wait_send()
    for c in range(tiles):
        part_copy(c).wait_send()


def fused(dims, images, img_pair, texts, txt_pair, gain, perm, right_blocks, left_blocks):
    nb, nn, nw = dims
    group = nn * nw
    t_rows, width = texts.shape
    r_rows = images.shape[0] // group
    two = 2 * r_rows
    block_count, size = right_blocks.shape[:2]
    tiles = 4
    vmem = pl.BlockSpec(memory_space=pltpu.VMEM)
    hbm = pl.BlockSpec(memory_space=pltpu.HBM)
    dma = pltpu.SemaphoreType.DMA
    grad, loss = pl.pallas_call(
        functools.partial(fused_kernel, dims),
        out_shape=(
            jax.ShapeDtypeStruct((r_rows, width), BF16),
            jax.ShapeDtypeStruct((1, images.shape[0]), F32),
        ),
        in_specs=[hbm] * 8,
        out_specs=(vmem, vmem),
        scratch_shapes=[
            pltpu.VMEM((1, images.shape[0]), jnp.int32),
            pltpu.VMEM((1, t_rows), jnp.int32),
            pltpu.VMEM((1, width), F32),
            pltpu.VMEM((1, width), jnp.int32),
            pltpu.VMEM(right_blocks.shape, BF16),
            pltpu.VMEM(left_blocks.shape, BF16),
            pltpu.VMEM((two, width), BF16),
            pltpu.VMEM((nw, block_count, size, 2 * size), BF16),
            pltpu.VMEM((nb, 4, t_rows, width), BF16),
            pltpu.VMEM((nb, 4, 1, 4 * t_rows), jnp.int32),
            pltpu.VMEM((two, width), BF16),
            pltpu.VMEM((two, width), BF16),
            pltpu.VMEM((two, width), BF16),
            pltpu.VMEM((two, width), BF16),
            pltpu.VMEM((nb, two, 4 * t_rows), F32),
            pltpu.VMEM((two, nb * 4 * t_rows), BF16),
            pltpu.VMEM((group, 8, 128), F32),
            pltpu.VMEM((tiles, r_rows, width // tiles), BF16),
            pltpu.VMEM((tiles, r_rows, width // tiles), BF16),
            pltpu.VMEM((tiles, r_rows, width // tiles), F32),
            dma((9,)),
            dma((3,)),
            dma((nw,)),
            dma((nb, 5, PARTS)),
            dma((nb, 4, PARTS)),
            dma((nb, 5)),
            dma((nb, 4)),
            dma((group - 1,)),
            dma((group,)),
            dma((tiles,)),
            dma((tiles,)),
        ],
        compiler_params=pltpu.CompilerParams(
            collective_id=0, has_side_effects=True, vmem_limit_bytes=VMEM_LIMIT
        ),
    )(
        images, img_pair[None], texts, txt_pair[None], gain[None], perm[None], right_blocks, left_blocks
    )
    return grad, loss[0]


def monarch(images, gain, perm, right_full, left_full):
    row_count, width = images.shape
    block_count, block_size = (right_full.shape[0], right_full.shape[1])
    values = images.astype(jnp.float32)
    row_mean = jnp.mean(values, axis=1, keepdims=True)
    centered = values - row_mean
    row_var = jnp.mean(centered * centered, axis=1, keepdims=True)
    normed = (centered * lax.rsqrt(row_var + 1e-05) * gain).astype(jnp.bfloat16)
    inner_mixed = jnp.einsum(
        "rke,kec->rkc",
        normed.reshape(row_count, block_count, block_size),
        right_full,
        preferred_element_type=jnp.float32,
    )
    active = (
        jax.nn.gelu(inner_mixed, approximate=True).astype(jnp.bfloat16).reshape(row_count, width)
    )
    permuted = jnp.take(active, perm, axis=1)
    outer_mixed = jnp.einsum(
        "rke,kec->rkc",
        permuted.reshape(row_count, block_count, block_size),
        left_full,
        preferred_element_type=jnp.float32,
    )
    return (values + outer_mixed.reshape(row_count, width)).astype(jnp.bfloat16)


def per_device(images, img_pair, texts, txt_pair, gain, perm, right_blocks, left_blocks):
    right_full, left_full = (
        lax.all_gather(right_blocks, "weight", axis=0, tiled=True),
        lax.all_gather(left_blocks, "weight", axis=0, tiled=True),
    )
    embedded = monarch(images, gain, perm, right_full, left_full)
    gathered, gathered_pair = (
        lax.all_gather(texts, "batch", axis=0, tiled=True),
        lax.all_gather(txt_pair, "batch", axis=0, tiled=True),
    )
    logit_scale = LOGIT_GAIN / math.sqrt(images.shape[1])
    scores = (
        jnp.einsum("rd,cd->rc", embedded, gathered, preferred_element_type=jnp.float32)
        * logit_scale
    )
    matches = (img_pair[:, None] == gathered_pair[None, :]).astype(jnp.float32)
    local_max = jnp.max(scores, axis=1)
    local_pos = jnp.sum(matches * scores, axis=1)
    row_max = lax.pmax(local_max, ("neg", "weight"))
    shifted = jnp.exp(scores - row_max[:, None])
    totals, positive = lax.psum((jnp.sum(shifted, axis=1), local_pos), ("neg", "weight"))
    row_loss = row_max + jnp.log(totals) - positive
    dscore = (shifted / totals[:, None] - matches).astype(jnp.bfloat16)
    grad_sum = lax.psum_scatter(
        jnp.dot(dscore, gathered, preferred_element_type=jnp.float32),
        ("neg", "weight"),
        scatter_dimension=0,
        tiled=True,
    )
    grad_img = grad_sum.astype(jnp.bfloat16)
    return (grad_img, row_loss)


def solution(mesh):
    dims = tuple(mesh.shape[axis] for axis in ("batch", "neg", "weight"))

    def body(images, img_pair, texts, txt_pair, gain, perm, right_blocks, left_blocks):
        args = (images, img_pair, texts, txt_pair, gain, perm, right_blocks, left_blocks)
        rows = images.shape[0] // math.prod(dims[1:])
        if (
            dims[1:] == (2, 4) and 2 <= dims[0] <= 8 and texts.shape[0] == 16 * PARTS == rows
            and 2 * rows <= 128
        ):
            return fused(dims, *args)
        return per_device(*args)

    return jax.shard_map(
        body,
        mesh=mesh,
        in_specs=(
            P("batch", None),
            P("batch"),
            P(("batch", "neg", "weight"), None),
            P(("batch", "neg", "weight")),
            P(),
            P(),
            P("weight", None, None),
            P("weight", None, None),
        ),
        out_specs=(P(("batch", "neg", "weight"), None), P("batch")),
        check_vma=False,
    )
```

time: 41.5 us -> 36.2 us (0.87)
  Pallas kernels: 38.5 us -> 33.3 us
    pallas_call x1, Pallas kernels: 38.5 us -> 33.3 us  [fused(): pl.pallas_call(functools.partial(fused_kernel, dims), out_shape=(jax.Shap...]
where the time goes in v1:
time: 36.2 us; the launch traced here: 36 us
  Pallas kernels  33.3 us (92%)
  local copies, waits for them, and re-layouts  2.14 us (6%)
  between operations  0.65 us (2%)
    pallas_call x1, Pallas kernels, fused(): pl.pallas_call(functools.partial(fused_kernel, dims), out_shape=(jax.Shap...  33.3 us
    unnamed x4, local copies, waits for them, and re-layouts  2.14 us

profile of v1, /device:TPU:0, one launch (start us, length us, event | category | flops | bytes accessed | tf_op | source)
XLA Modules:
  0.0 36.0 jit_solution(4392391283326008003)
XLA Ops:
  0.6 33.3 %shard_map.95 = (bf16[32,2048]{1,0:T(8,128)(2,1)}, f32[1,256]{1,0:T(1,128)}) custom-call(bf16[256,2048]{1,0:T(8,128)(2,1)} %images_hbm.1, s32[1,256]{1,0:T(1,128)} %bitcast.7, bf16[32,2048]{1,0:T(8,128)(2,1)} %texts_ref.1, s32[1,32]{1,0:T(1,128)} %bitcast.9, f32[1,2048]{1,0:T(1,128)} %bitcast.5, s32[1,2048]{1,0:T(1,128)} %bitcast.6, ...), custom_call_target="tpu_custom_call" | custom-call | tf_op jit(solution)/shard_map/pallas_call | solution.py:412
  33.9 0.0 copy-start
  33.9 1.6 %copy.12 = bf16[32,2048]{1,0:T(8,128)(2,1)} copy(bf16[32,2048]{1,0:T(8,128)(2,1)} %get-tuple-element.8) | data formatting | bytes 262144
  35.5 0.0 copy-done
  35.5 0.6 %copy.13 = f32[256]{0:T(256)} copy(f32[256]{0:T(256)S(1)} %bitcast.8) | data formatting | bytes 2048
Async XLA Ops:
  33.9 1.6 %copy-start = (f32[1,256]{1,0:T(1,128)S(1)}, f32[1,256]{1,0:T(1,128)}, u32[]{:S(2)}) copy-start(f32[1,256]{1,0:T(1,128)} %get-tuple-element.5) | copy-start | bytes 3076

commit v2 on v1

--- a/solution.py
+++ b/solution.py
@@ -12,7 +12,7 @@
 MESH = pl.DeviceIdType.MESH
 F32, BF16 = jnp.float32, jnp.bfloat16
 PARTS = 2
-VMEM_LIMIT = 67_043_328
+VMEM_LIMIT = 48 * 2**20
 
 
 def plane_orders(count):
@@ -381,7 +381,7 @@
     for x_o in range(2):
         both = pair_loss(2 * x_o + 1, nw + 2 * x_o + 1)
         losses[2 * x_o + 1], losses[nw + 2 * x_o + 1] = both[:, :r_rows], both[:, r_rows:two]
-    loss_ref[...] = jnp.concatenate([losses[i] for i in range(nn * nw)], axis=1)
+    loss_ref[...] = jnp.concatenate([losses[i] for i in range(nn * nw)], axis=1)[0]
 
     for c in range(tiles):
         part_copy(c).wait_recv()
@@ -413,7 +413,7 @@
         functools.partial(fused_kernel, dims),
         out_shape=(
             jax.ShapeDtypeStruct((r_rows, width), BF16),
-            jax.ShapeDtypeStruct((1, images.shape[0]), F32),
+            jax.ShapeDtypeStruct((images.shape[0],), F32),
         ),
         in_specs=[hbm] * 8,
         out_specs=(vmem, vmem),
@@ -454,9 +454,33 @@
             collective_id=0, has_side_effects=True, vmem_limit_bytes=VMEM_LIMIT
         ),
     )(
-        images, img_pair[None], texts, txt_pair[None], gain[None], perm[None], right_blocks, left_blocks
-    )
-    return grad, loss[0]
+        *[
+            pltpu.with_memory_space_constraint(value, pltpu.HBM)
+            for value in (images, img_pair[None], texts, txt_pair[None], gain[None], perm[None], right_blocks, left_blocks)
+        ]
+    )
+    return pl.pallas_call(
+        hand_out,
+        out_shape=(
+            jax.ShapeDtypeStruct((r_rows, width), BF16),
+            jax.ShapeDtypeStruct((images.shape[0],), F32),
+        ),
+        in_specs=[vmem, vmem],
+        out_specs=(hbm, hbm),
+        scratch_shapes=[dma((2,))],
+        compiler_params=pltpu.CompilerParams(vmem_limit_bytes=2**20),
+    )(grad, loss)
+
+
+def hand_out(grad_ref, loss_ref, grad_hbm, loss_hbm, sem):
+    copies = [
+        pltpu.make_async_copy(grad_ref, grad_hbm, sem.at[0]),
+        pltpu.make_async_copy(loss_ref, loss_hbm, sem.at[1]),
+    ]
+    for copy in copies:
+        copy.start()
+    for copy in copies:
+        copy.wait()
 
 
 def monarch(images, gain, perm, right_full, left_full):

time: 36.2 us -> 34.1 us (0.942)
  local copies, waits for them, and re-layouts: 2.14 us -> 0 us
    unnamed x4 -> x0, local copies, waits for them, and re-layouts: 2.14 us -> none
    pallas_call x0 -> x1, Pallas kernels: none -> 0.68 us  [fused(): pl.pallas_call(hand_out, out_shape=(jax.ShapeDtypeStruct((r_rows, width),...]
    pallas_call x1, Pallas kernels: 33.3 us -> 32.6 us  [fused(): pl.pallas_call(functools.partial(fused_kernel, dims), out_shape=(jax.Shap...]
where the time goes in v2:
time: 34.1 us; the launch traced here: 33.9 us
  Pallas kernels  33.3 us (98%)
  between operations  0.64 us (2%)
    pallas_call x1, Pallas kernels, fused(): pl.pallas_call(functools.partial(fused_kernel, dims), out_shape=(jax.Shap...  32.6 us

profile of v2, /device:TPU:0, one launch (start us, length us, event | category | flops | bytes accessed | tf_op | source)
XLA Modules:
  0.0 33.9 jit_solution(14419855401614894920)
XLA Ops:
  0.6 32.6 %shard_map.95 = (bf16[32,2048]{1,0:T(8,128)(2,1)S(1)}, f32[256]{0:T(256)S(1)}) custom-call(bf16[256,2048]{1,0:T(8,128)(2,1)} %images_hbm.1, s32[1,256]{1,0:T(1,128)} %bitcast.6, bf16[32,2048]{1,0:T(8,128)(2,1)} %texts_ref.1, s32[1,32]{1,0:T(1,128)} %bitcast.7, f32[1,2048]{1,0:T(1,128)} %bitcast.4, s32[1,2048]{1,0:T(1,128)} %bitcast.5, ...), custom_call_target="tpu_custom_call" | custom-call | tf_op jit(solution)/shard_map/pallas_call | solution.py:412
  33.3 0.7 %shard_map.96 = (bf16[32,2048]{1,0:T(8,128)(2,1)}, f32[256]{0:T(256)}) custom-call(bf16[32,2048]{1,0:T(8,128)(2,1)S(1)} %get-tuple-element.4.grad_ref, f32[256]{0:T(256)S(1)} %get-tuple-element.5.loss_ref), custom_call_target="tpu_custom_call" | custom-call | tf_op jit(solution)/shard_map/pallas_call | solution.py:462
